TPU v7x, 32 devices: a whole 2x2x4 slice. The times are simulated.
32 devices in a mesh: group: 2 (over y), replica: 16 (over z, x, core).
Axes of the slice: x: 2, y: 2, z: 4, core: 2. Of those that a mesh axis runs over, the one named last changes fastest.
Arguments:
- tokens: bfloat16 [6144, 960], P(('group', 'replica')), may hold values from -6 to 6
- seq_lens: int32 [32, 4], P(('group', 'replica')), may hold values from 1 to 96, 192 in all within a row
- cotangent: bfloat16 [6144, 960], P(('group', 'replica')), may hold values from -6 to 6
- norm1_gain: bfloat16 [960], P('group'), may hold values from 0.25 to 1.75
- w_query: bfloat16 [960, 960], P('group'), may hold values from -0.1875 to 0.1875
- key_weight: bfloat16 [960, 320], P('group'), may hold values from -0.1875 to 0.1875
- value_weight: bfloat16 [960, 320], P('group'), may hold values from -0.1875 to 0.1875
- w_output: bfloat16 [960, 960], P('group'), may hold values from -0.5 to 0.5
- norm2_gain: bfloat16 [960], P('group'), may hold values from 0.25 to 1.75
- w_gate: bfloat16 [960, 2560], P(None, 'group'), may hold values from -0.1875 to 0.1875
- w_up: bfloat16 [960, 2560], P(None, 'group'), may hold values from -0.1875 to 0.1875
- w_down: bfloat16 [2560, 960], P('group'), may hold values from -0.125 to 0.125
Outputs:
- layer_out: bfloat16 [6144, 960], P(('group', 'replica'))
- tokens_grad: float32 [6144, 960], P(('group', 'replica'))
- norm1_gain_grad: float32 [960], P('group')
- w_query_grad: float32 [960, 960], P('group')
- w_key_grad: float32 [960, 320], P('group')
- w_value_grad: float32 [960, 320], P('group')
- w_output_grad: float32 [960, 960], P('group')
- norm2_gain_grad: float32 [960], P('group')
- w_gate_grad: float32 [960, 2560], P(None, 'group')
- w_up_grad: float32 [960, 2560], P(None, 'group')
- w_down_grad: float32 [2560, 960], P('group')
Inputs may be any that keep to these rules, and one draw needn't show every extreme that they name: `seq_lens`: each device's row holds the lengths of its 4 sequences, which add up to 192; the longest in every row is 96.
All inputs are finite; a program needn't handle non-finite values.
Results may differ from a plain program's by a relative error of at most 0.023.
Values may be sent and summed in bfloat16 or wider, within the bound.
A program may use at most 192 MiB of HBM per device.

v0:
```python
import math
import jax
import jax.numpy as jnp
from jax import lax
from jax.sharding import PartitionSpec as P

QUERY_HEADS = 15
KEY_VALUE_HEADS = 5
HEAD_SIZE = 64
EPS = 1e-05


def matrix_product(left, right):
    return jnp.dot(left, right, preferred_element_type=jnp.float32)


def left_t_product(left, right):
    return lax.dot_general(
        left, right, (((0,), (0,)), ((), ())), preferred_element_type=jnp.float32
    )


def right_t_product(left, right):
    return lax.dot_general(
        left, right, (((1,), (1,)), ((), ())), preferred_element_type=jnp.float32
    )


def mixed_einsum(form, left, right):
    return jnp.einsum(form, left, right, preferred_element_type=jnp.float32)


def sequence_tables(lengths, token_count):
    ends = jnp.cumsum(lengths)
    starts = ends - lengths
    indices = jnp.arange(token_count, dtype=jnp.int32)
    seq_of = jnp.sum((indices[:, None] >= ends[None, :]).astype(jnp.int32), axis=1)
    onehot = (seq_of[:, None] == jnp.arange(lengths.shape[0], dtype=jnp.int32)[None, :]).astype(
        jnp.int32
    )
    position = indices - jnp.sum(onehot * starts[None, :], axis=1)
    half_dim = HEAD_SIZE // 2
    freqs = 10000.0 ** (-(jnp.arange(half_dim, dtype=jnp.float32) * 2.0 / HEAD_SIZE))
    angles = position.astype(jnp.float32)[:, None] * freqs[None, :]
    visible = (seq_of[:, None] == seq_of[None, :]) & (indices[None, :] <= indices[:, None])
    return (jnp.cos(angles), jnp.sin(angles), visible)


def apply_rotary(values, cosine_table, sine_table):
    half_dim = values.shape[-1] // 2
    first_half = values[..., :half_dim]
    second_half = values[..., half_dim:]
    cos_b = cosine_table[:, None, :]
    sin_b = sine_table[:, None, :]
    return jnp.concatenate(
        [first_half * cos_b - second_half * sin_b, second_half * cos_b + first_half * sin_b],
        axis=-1,
    )


def rotary_backward(values, cosine_table, sine_table):
    half_dim = values.shape[-1] // 2
    first_half = values[..., :half_dim]
    second_half = values[..., half_dim:]
    cos_b = cosine_table[:, None, :]
    sin_b = sine_table[:, None, :]
    return jnp.concatenate(
        [first_half * cos_b + second_half * sin_b, second_half * cos_b - first_half * sin_b],
        axis=-1,
    )


def rms_scale(resid, gain):
    inv_rms = lax.rsqrt(jnp.mean(resid * resid, axis=-1, keepdims=True) + EPS)
    return ((resid * inv_rms * gain.astype(jnp.float32)).astype(jnp.bfloat16), inv_rms)


def rms_back(d_normed, resid, inv_rms, gain):
    scaled = d_normed * gain.astype(jnp.float32)
    d_resid = inv_rms * scaled - resid * inv_rms**3 * jnp.mean(
        scaled * resid, axis=-1, keepdims=True
    )
    d_gain = jnp.sum(d_normed * resid * inv_rms, axis=0)
    return (d_resid, d_gain)


def masked_scores(query_rotated, key_rotated, visible):
    token_count = query_rotated.shape[0]
    query_grouped = query_rotated.reshape(
        token_count, KEY_VALUE_HEADS, QUERY_HEADS // KEY_VALUE_HEADS, HEAD_SIZE
    )
    scores = mixed_einsum("qhgd,khd->hgqk", query_grouped, key_rotated) * (
        1.0 / math.sqrt(HEAD_SIZE)
    )
    return (jnp.where(visible[None, None], scores, -1e30), query_grouped)


def attention(query_rotated, key_rotated, value_row_block, visible):
    token_count = query_rotated.shape[0]
    scores, query_grouped = masked_scores(query_rotated, key_rotated, visible)
    top = jnp.max(scores, axis=-1, keepdims=True)
    expo = jnp.exp(scores - top)
    total = jnp.sum(expo, axis=-1, keepdims=True)
    log_total = top + jnp.log(total)
    probs = (expo / total).astype(jnp.bfloat16)
    mixed = mixed_einsum("hgqk,khd->qhgd", probs, value_row_block)
    return (mixed.reshape(token_count, QUERY_HEADS * HEAD_SIZE).astype(jnp.bfloat16), log_total)


def attention_back(
    query_rotated,
    key_rotated,
    value_row_block,
    attention_mixture,
    mixture_gradient,
    log_total,
    visible,
):
    token_count = query_rotated.shape[0]
    scores, query_grouped = masked_scores(query_rotated, key_rotated, visible)
    weights_f = jnp.exp(scores - log_total)
    probs = weights_f.astype(jnp.bfloat16)
    mixture_gradient_grouped = mixture_gradient.reshape(
        token_count, KEY_VALUE_HEADS, QUERY_HEADS // KEY_VALUE_HEADS, HEAD_SIZE
    )
    mixture_grouped = attention_mixture.reshape(
        token_count, KEY_VALUE_HEADS, QUERY_HEADS // KEY_VALUE_HEADS, HEAD_SIZE
    )
    value_gradient = mixed_einsum("hgqk,qhgd->khd", probs, mixture_gradient_grouped)
    d_probs = mixed_einsum("qhgd,khd->hgqk", mixture_gradient_grouped, value_row_block)
    delta = mixed_einsum("qhgd,qhgd->hgq", mixture_gradient_grouped, mixture_grouped)[..., None]
    d_scores = (weights_f * (d_probs - delta) * (1.0 / math.sqrt(HEAD_SIZE))).astype(jnp.bfloat16)
    d_query = mixed_einsum("hgqk,khd->qhgd", d_scores, key_rotated).reshape(
        token_count, QUERY_HEADS, HEAD_SIZE
    )
    key_gradient = mixed_einsum("hgqk,qhgd->khd", d_scores, query_grouped)
    return (d_query, key_gradient, value_gradient)


def forward_pass(block, lengths, weights):
    gain_one, w_query, key_weight, value_weight, w_output, gain_two, w_gate, w_up, w_down = weights
    token_count = block.shape[0]
    cosine_table, sine_table, visible = sequence_tables(lengths, token_count)
    resid_in = block.astype(jnp.float32)
    first_normed_input, inv_rms_one = rms_scale(resid_in, gain_one)
    query_rotated = apply_rotary(
        matrix_product(first_normed_input, w_query).reshape(token_count, QUERY_HEADS, HEAD_SIZE),
        cosine_table,
        sine_table,
    ).astype(jnp.bfloat16)
    key_rotated = apply_rotary(
        matrix_product(first_normed_input, key_weight).reshape(
            token_count, KEY_VALUE_HEADS, HEAD_SIZE
        ),
        cosine_table,
        sine_table,
    ).astype(jnp.bfloat16)
    value_row_block = (
        matrix_product(first_normed_input, value_weight)
        .astype(jnp.bfloat16)
        .reshape(token_count, KEY_VALUE_HEADS, HEAD_SIZE)
    )
    attention_mixture, log_total = attention(query_rotated, key_rotated, value_row_block, visible)
    resid_mid = resid_in + matrix_product(attention_mixture, w_output)
    normed_two, inv_rms_two = rms_scale(resid_mid, gain_two)
    gate_pre = matrix_product(normed_two, w_gate)
    up_pre = matrix_product(normed_two, w_up)
    hidden = (jax.nn.silu(gate_pre) * up_pre).astype(jnp.bfloat16)
    resid_out = resid_mid + matrix_product(hidden, w_down)
    saved = (
        resid_in,
        first_normed_input,
        inv_rms_one,
        query_rotated,
        key_rotated,
        value_row_block,
        attention_mixture,
        log_total,
        resid_mid,
        normed_two,
        inv_rms_two,
        gate_pre,
        up_pre,
        hidden,
        cosine_table,
        sine_table,
        visible,
    )
    return (resid_out.astype(jnp.bfloat16), saved)


def mlp_backward(d_out, saved, weights):
    gain_one, w_query, key_weight, value_weight, w_output, gain_two, w_gate, w_up, w_down = weights
    resid_mid, normed_two, inv_rms_two, gate_pre, up_pre, hidden = saved[8:14]
    d_out_b = d_out.astype(jnp.bfloat16)
    grad_down = left_t_product(hidden, d_out_b)
    d_hidden = right_t_product(d_out_b, w_down)
    sigma = jax.nn.sigmoid(gate_pre)
    d_gate = (d_hidden * up_pre * sigma * (1.0 + gate_pre * (1.0 - sigma))).astype(jnp.bfloat16)
    d_up = (d_hidden * gate_pre * sigma).astype(jnp.bfloat16)
    grad_gate = left_t_product(normed_two, d_gate)
    grad_up = left_t_product(normed_two, d_up)
    d_normed_two = right_t_product(d_gate, w_gate) + right_t_product(d_up, w_up)
    d_resid_part, grad_gain_two = rms_back(d_normed_two, resid_mid, inv_rms_two, gain_two)
    return (d_out + d_resid_part, (grad_gain_two, grad_gate, grad_up, grad_down))


def attn_backward(d_resid_mid, saved, weights):
    gain_one, w_query, key_weight, value_weight, w_output, gain_two, w_gate, w_up, w_down = weights
    (
        resid_in,
        first_normed_input,
        inv_rms_one,
        query_rotated,
        key_rotated,
        value_row_block,
        attention_mixture,
        log_total,
    ) = saved[:8]
    cosine_table, sine_table, visible = saved[14:]
    token_count = resid_in.shape[0]
    d_mid_b = d_resid_mid.astype(jnp.bfloat16)
    grad_output = left_t_product(attention_mixture, d_mid_b)
    mixture_gradient = right_t_product(d_mid_b, w_output).astype(jnp.bfloat16)
    d_query, key_gradient, value_gradient = attention_back(
        query_rotated,
        key_rotated,
        value_row_block,
        attention_mixture,
        mixture_gradient,
        log_total,
        visible,
    )
    d_query_b = (
        rotary_backward(d_query, cosine_table, sine_table)
        .reshape(token_count, QUERY_HEADS * HEAD_SIZE)
        .astype(jnp.bfloat16)
    )
    key_gradient_block = (
        rotary_backward(key_gradient, cosine_table, sine_table)
        .reshape(token_count, KEY_VALUE_HEADS * HEAD_SIZE)
        .astype(jnp.bfloat16)
    )
    value_gradient_block = value_gradient.reshape(token_count, KEY_VALUE_HEADS * HEAD_SIZE).astype(
        jnp.bfloat16
    )
    grad_query = left_t_product(first_normed_input, d_query_b)
    grad_key = left_t_product(first_normed_input, key_gradient_block)
    grad_value = left_t_product(first_normed_input, value_gradient_block)
    d_normed_one = (
        right_t_product(d_query_b, w_query)
        + right_t_product(key_gradient_block, key_weight)
        + right_t_product(value_gradient_block, value_weight)
    )
    d_resid_part, grad_gain_one = rms_back(d_normed_one, resid_in, inv_rms_one, gain_one)
    return (
        d_resid_mid + d_resid_part,
        (grad_gain_one, grad_query, grad_key, grad_value, grad_output),
    )


def local(
    tokens,
    seq_lens,
    cotangent,
    norm1_gain,
    w_query,
    key_weight,
    value_weight,
    w_output,
    norm2_gain,
    w_gate,
    w_up,
    w_down,
):
    weights = (
        lax.all_gather(norm1_gain, "group", axis=0, tiled=True),
        lax.all_gather(w_query, "group", axis=0, tiled=True),
        lax.all_gather(key_weight, "group", axis=0, tiled=True),
        lax.all_gather(value_weight, "group", axis=0, tiled=True),
        lax.all_gather(w_output, "group", axis=0, tiled=True),
        lax.all_gather(norm2_gain, "group", axis=0, tiled=True),
        lax.all_gather(w_gate, "group", axis=1, tiled=True),
        lax.all_gather(w_up, "group", axis=1, tiled=True),
        lax.all_gather(w_down, "group", axis=0, tiled=True),
    )
    layer_out, saved = forward_pass(tokens, seq_lens[0], weights)
    weights = (
        lax.all_gather(norm1_gain, "group", axis=0, tiled=True),
        lax.all_gather(w_query, "group", axis=0, tiled=True),
        lax.all_gather(key_weight, "group", axis=0, tiled=True),
        lax.all_gather(value_weight, "group", axis=0, tiled=True),
        lax.all_gather(w_output, "group", axis=0, tiled=True),
        lax.all_gather(norm2_gain, "group", axis=0, tiled=True),
        lax.all_gather(w_gate, "group", axis=1, tiled=True),
        lax.all_gather(w_up, "group", axis=1, tiled=True),
        lax.all_gather(w_down, "group", axis=0, tiled=True),
    )
    factor = 1.0 / math.sqrt(
        float(tokens.shape[0] * lax.axis_size("group") * lax.axis_size("replica"))
    )
    d_resid_mid, mlp_grads = mlp_backward(cotangent.astype(jnp.float32), saved, weights)
    tokens_grad, attn_grads = attn_backward(d_resid_mid, saved, weights)
    parts = (
        lax.psum_scatter(
            attn_grads[0].astype(jnp.bfloat16), "group", scatter_dimension=0, tiled=True
        ).astype(jnp.float32),
        lax.psum_scatter(
            attn_grads[1].astype(jnp.bfloat16), "group", scatter_dimension=0, tiled=True
        ).astype(jnp.float32),
        lax.psum_scatter(
            attn_grads[2].astype(jnp.bfloat16), "group", scatter_dimension=0, tiled=True
        ).astype(jnp.float32),
        lax.psum_scatter(
            attn_grads[3].astype(jnp.bfloat16), "group", scatter_dimension=0, tiled=True
        ).astype(jnp.float32),
        lax.psum_scatter(
            attn_grads[4].astype(jnp.bfloat16), "group", scatter_dimension=0, tiled=True
        ).astype(jnp.float32),
        lax.psum_scatter(
            mlp_grads[0].astype(jnp.bfloat16), "group", scatter_dimension=0, tiled=True
        ).astype(jnp.float32),
        lax.psum_scatter(
            mlp_grads[1].astype(jnp.bfloat16), "group", scatter_dimension=1, tiled=True
        ).astype(jnp.float32),
        lax.psum_scatter(
            mlp_grads[2].astype(jnp.bfloat16), "group", scatter_dimension=1, tiled=True
        ).astype(jnp.float32),
        lax.psum_scatter(
            mlp_grads[3].astype(jnp.bfloat16), "group", scatter_dimension=0, tiled=True
        ).astype(jnp.float32),
    )
    totals = (
        lax.psum(parts[0].astype(jnp.bfloat16), "replica").astype(jnp.float32),
        lax.psum(parts[1].astype(jnp.bfloat16), "replica").astype(jnp.float32),
        lax.psum(parts[2].astype(jnp.bfloat16), "replica").astype(jnp.float32),
        lax.psum(parts[3].astype(jnp.bfloat16), "replica").astype(jnp.float32),
        lax.psum(parts[4].astype(jnp.bfloat16), "replica").astype(jnp.float32),
        lax.psum(parts[5].astype(jnp.bfloat16), "replica").astype(jnp.float32),
        lax.psum(parts[6].astype(jnp.bfloat16), "replica").astype(jnp.float32),
        lax.psum(parts[7].astype(jnp.bfloat16), "replica").astype(jnp.float32),
        lax.psum(parts[8].astype(jnp.bfloat16), "replica").astype(jnp.float32),
    )
    return (
        layer_out,
        tokens_grad,
        totals[0] * factor,
        totals[1] * factor,
        totals[2] * factor,
        totals[3] * factor,
        totals[4] * factor,
        totals[5] * factor,
        totals[6] * factor,
        totals[7] * factor,
        totals[8] * factor,
    )


def solution(mesh):
    in_specs = (
        P(("group", "replica"), None),
        P(("group", "replica"), None),
        P(("group", "replica"), None),
        P("group"),
        P("group", None),
        P("group", None),
        P("group", None),
        P("group", None),
        P("group"),
        P(None, "group"),
        P(None, "group"),
        P("group", None),
    )
    out_specs = (
        P(("group", "replica"), None),
        P(("group", "replica"), None),
        P("group"),
        P("group", None),
        P("group", None),
        P("group", None),
        P("group", None),
        P("group"),
        P(None, "group"),
        P(None, "group"),
        P("group", None),
    )
    return jax.shard_map(local, mesh=mesh, in_specs=in_specs, out_specs=out_specs, check_vma=False)
```

profile of v0, /device:TPU:0, one launch (start us, length us, event | category | flops | bytes accessed | tf_op | source)
XLA Modules:
  0.0 832.0 jit_solution(7892637476535821670)
XLA Ops:
  12.9 5.9 all-reduce.7
  18.8 17.0 %all-gather.1 = bf16[2,480,320]{1,2,0:T(8,128)(2,1)S(1)} all-gather(bf16[1,480,320]{1,2,0:T(8,128)(2,1)S(1)} %bitcast.134), channel_id=1, replica_groups=mesh['group'=2,'replica'=16] {'group'}, dimensions={0}, use_global_device_ids=true | all-gather | bytes 921600 | tf_op jit(solution)/shard_map/all_gather | solution.py:279
  37.1 17.9 %all-gather = bf16[2,480,320]{1,2,0:T(8,128)(2,1)S(1)} all-gather(bf16[1,480,320]{1,2,0:T(8,128)(2,1)S(1)} %bitcast.135), channel_id=1, replica_groups=mesh['group'=2,'replica'=16] {'group'}, dimensions={0}, use_global_device_ids=true | all-gather | bytes 921600 | tf_op jit(solution)/shard_map/all_gather | solution.py:280
  59.1 2.6 fusion.38
  62.6 1.5 fusion.44
  65.2 1.4 fusion.9
  66.6 24.5 %all-gather.10.cloned.1.call-done = bf16[960,960]{1,0:T(8,128)(2,1)} async-done(((bf16[480,960]{1,0:T(8,128)(2,1)}), bf16[960,960]{1,0:T(8,128)(2,1)}) %all-gather.10.cloned.1.call-update) | async-done | bytes 1843216 | tf_op jit(solution)/shard_map/all_gather | solution.py:281
  91.1 2.4 multiply_reduce_fusion.2
  95.3 62.2 %all-gather.14.cloned.1.call-done = bf16[960,2560]{1,0:T(8,128)(2,1)} async-done(((bf16[960,1280]{1,0:T(8,128)(2,1)}), bf16[960,2560]{1,0:T(8,128)(2,1)}) %all-gather.14.cloned.1.call-update) | async-done | bytes 4915216 | tf_op jit(solution)/shard_map/all_gather | solution.py:284
  157.5 5.0 fusion.46
  162.5 61.3 %all-gather.12.cloned.1.call-done = bf16[960,2560]{1,0:T(8,128)(2,1)} async-done(((bf16[960,1280]{1,0:T(8,128)(2,1)}), bf16[960,2560]{1,0:T(8,128)(2,1)}) %all-gather.12.cloned.1.call-update) | async-done | bytes 4915216 | tf_op jit(solution)/shard_map/all_gather | solution.py:283
  223.8 5.0 fusion.45
  228.8 61.3 %all-gather.16.cloned.1.call-done = bf16[2560,960]{0,1:T(8,128)(2,1)} async-done(((bf16[1280,960]{0,1:T(8,128)(2,1)}), bf16[2560,960]{0,1:T(8,128)(2,1)}) %all-gather.16.cloned.1.call-update) | async-done | bytes 4915216 | tf_op jit(solution)/shard_map/all_gather | solution.py:285
  290.1 6.4 multiply_convert_fusion
  296.5 1.6 fusion.47
  298.2 4.8 multiply_reduce_fusion
  304.8 1.5 convolution_convert_fusion.7
  306.3 2.0 copy.65
  308.3 1.9 fusion.14
  310.2 1.3 convolution_convert_fusion.5
  311.4 2.3 copy.89
  313.8 1.4 fusion.17
  315.2 1.9 fusion.2
  319.4 1.2 copy.87
  320.6 1.9 convolution_convert_fusion.3
  322.7 1.3 fusion.30
  325.0 2.1 convolution_convert_fusion.4
  327.2 3.7 convolution_convert_fusion
  332.3 3.7 convolution_convert_fusion.1
  337.2 3.7 convolution_convert_fusion.2
  341.0 1.9 copy.90
  342.9 7.3 reduce-scatter.22.cloned.1.call-done
  350.2 1.9 copy.88
  352.0 31.5 %reduce-scatter.14.cloned.1.call-done = bf16[480,960]{1,0:T(8,128)(2,1)} async-done(((bf16[960,960]{1,0:T(8,128)(2,1)}), bf16[480,960]{1,0:T(8,128)(2,1)}) %reduce-scatter.14.cloned.1.call-update) | async-done | bytes 921616 | tf_op jit(solution)/shard_map/reduce_scatter | solution.py:317
  383.5 33.3 %reduce-scatter.12.cloned.1.call-done = bf16[480,960]{1,0:T(8,128)(2,1)} async-done(((bf16[960,960]{1,0:T(8,128)(2,1)}), bf16[480,960]{1,0:T(8,128)(2,1)}) %reduce-scatter.12.cloned.1.call-update) | async-done | bytes 921616 | tf_op jit(solution)/shard_map/reduce_scatter | solution.py:308
  416.8 65.0 %reduce-scatter.20.cloned.1.call-done = bf16[1280,960]{0,1:T(8,128)(2,1)} async-done(((bf16[2560,960]{0,1:T(8,128)(2,1)}), bf16[1280,960]{0,1:T(8,128)(2,1)}) %reduce-scatter.20.cloned.1.call-update) | async-done | bytes 2457616 | tf_op jit(solution)/shard_map/reduce_scatter | solution.py:329
  481.8 65.1 %reduce-scatter.18.cloned.1.call-done = bf16[960,1280]{1,0:T(8,128)(2,1)} async-done(((bf16[960,2560]{1,0:T(8,128)(2,1)}), bf16[960,1280]{1,0:T(8,128)(2,1)}) %reduce-scatter.18.cloned.1.call-update) | async-done | bytes 2457616 | tf_op jit(solution)/shard_map/reduce_scatter | solution.py:326
  546.9 65.0 %reduce-scatter.16.cloned.1.call-done = bf16[960,1280]{1,0:T(8,128)(2,1)} async-done(((bf16[960,2560]{1,0:T(8,128)(2,1)}), bf16[960,1280]{1,0:T(8,128)(2,1)}) %reduce-scatter.16.cloned.1.call-update) | async-done | bytes 2457616 | tf_op jit(solution)/shard_map/reduce_scatter | solution.py:323
  613.5 1.9 fusion.48
  616.5 4.9 all-reduce.6
  621.6 33.8 %all-reduce.4 = (bf16[480]{0:T(512)(128)(2,1)S(1)}, bf16[480]{0:T(512)(128)(2,1)S(1)}) all-reduce(bf16[480]{0:T(512)(128)(2,1)S(1)} %dynamic-slice.3, bf16[480]{0:T(512)(128)(2,1)S(1)} %dynamic-slice.5), channel_id=1, replica_groups=mesh['group'=2,'replica'=16] {'replica'}, use_global_device_ids=true, to_apply=%region_11.12 | all-reduce | flops 960 | bytes 3840 | tf_op jit(solution)/shard_map/psum | solution.py:334
  657.1 5.1 fusion.10
  662.3 148.8 %all-reduce.10.cloned.1.call-done = (bf16[480,960]{1,0:T(8,128)(2,1)}, bf16[480,320]{0,1:T(8,128)(2,1)}, bf16[480,320]{0,1:T(8,128)(2,1)}, bf16[480,960]{1,0:T(8...) async-done(((bf16[480,960]{1,0:T(8,128)(2,1)}, bf16[480,320]{0,1:T(8,128)(2,1)}, bf16[480,320]{0,1:T(8,128)(2,1)}, ...) | async-done | bytes 9830416 | tf_op jit(solution)/shard_map/psum | solution.py:335
  811.1 4.5 convert_multiply_fusion
  815.6 1.2 convert_multiply_fusion.11
  816.9 2.5 convert_multiply_fusion.3
  819.4 1.3 copy-done.19
  820.7 4.7 convert_multiply_fusion.1
  (176 shorter events, 25.5 us)
Async XLA Ops:
  7.2 51.9 %all-gather.8.cloned.1.call-start = ((), (), s32[]{:S(2)}) async-start(), calls=%async_computation.7 | async-start | bytes 2949120 | tf_op jit(solution)/shard_map/all_gather | solution.py:278
  7.9 83.2 %all-gather.10.cloned.1.call-start = ((), (), s32[]{:S(2)}) async-start(), calls=%async_computation.8 | async-start | bytes 2949120 | tf_op jit(solution)/shard_map/all_gather | solution.py:281
  8.7 148.8 %all-gather.14.cloned.1.call-start = ((), (), s32[]{:S(2)}) async-start(), calls=%async_computation.10 | async-start | bytes 7372800 | tf_op jit(solution)/shard_map/all_gather | solution.py:284
  9.4 1.8 copy-start.47
  9.4 3.0 copy-start.49
  9.4 3.3 copy-start.50
  9.4 9.4 %copy-start.39 = (bf16[480,320]{0,1:T(8,128)(2,1)S(1)}, bf16[480,320]{0,1:T(8,128)(2,1)}, u32[]{:S(2)}) copy-start(bf16[480,320]{0,1:T(8,128)(2,1)} %param.17) | copy-start | bytes 921604
  9.5 214.3 %all-gather.12.cloned.1.call-start = ((), (), s32[]{:S(2)}) async-start(), calls=%async_computation.9 | async-start | bytes 7372800 | tf_op jit(solution)/shard_map/all_gather | solution.py:283
  10.0 27.1 %copy-start.40 = (bf16[480,320]{0,1:T(8,128)(2,1)S(1)}, bf16[480,320]{0,1:T(8,128)(2,1)}, u32[]{:S(2)}) copy-start(bf16[480,320]{0,1:T(8,128)(2,1)} %param.18) | copy-start | bytes 921604
  10.0 280.0 %all-gather.16.cloned.1.call-start = ((), (), s32[]{:S(2)}) async-start(), calls=%async_computation.11 | async-start | bytes 7372800 | tf_op jit(solution)/shard_map/all_gather | solution.py:285
  10.6 330.4 %reduce-scatter.24.cloned.1.call-start = ((), (), s32[]{:S(2)}) async-start(), calls=%async_computation.18 | async-start | bytes 1105920
  37.1 21.3 %copy-start.14 = (bf16[960,320]{0,1:T(8,128)(2,1)}, bf16[960,320]{0,1:T(8,128)(2,1)S(1)}, u32[]{:S(2)}) copy-start(bf16[960,320]{0,1:T(8,128)(2,1)S(1)} %reshape.227) | copy-start | bytes 1843204
  56.3 5.4 copy-start.16
  56.9 7.7 copy-start.36
  58.0 3.9 copy-start.33
  59.1 3.4 copy-start.37
  59.1 3.4 copy-start.38
  61.9 2.2 copy-start.31
  66.6 26.9 %copy-start.44 = (f32[5,3,192]{2,1,0:T(4,128)S(1)}, f32[5,3,192]{2,1,0:T(4,128)}, u32[]{:S(2)}) copy-start(f32[5,3,192]{2,1,0:T(4,128)} %copy-done.43) | copy-start | bytes 34564
  66.6 26.9 %copy-start.46 = (f32[5,3,192]{2,1,0:T(4,128)S(1)}, f32[5,3,192]{2,1,0:T(4,128)}, u32[]{:S(2)}) copy-start(f32[5,3,192]{2,1,0:T(4,128)} %copy-done.45) | copy-start | bytes 34564
  290.1 6.4 copy-start.2
  296.5 1.7 copy-start.8
  298.2 4.8 copy-start.21
  303.0 1.8 copy-start.11
  313.7 36.4 %reduce-scatter.22.cloned.1.call-start = ((), (), s32[]{:S(2)}) async-start(), calls=%async_computation.17 | async-start | bytes 1105920
  313.8 4.4 copy-start.30
  313.8 4.4 copy-start.32
  315.2 3.6 copy-start.34
  318.2 2.4 copy-start.6
  318.2 2.4 copy-start.13
  320.5 2.1 copy-start.4
  320.6 62.9 %reduce-scatter.14.cloned.1.call-start = ((), (), s32[]{:S(2)}) async-start(), calls=%async_computation.13 | async-start | bytes 2949120 | tf_op jit(solution)/shard_map/reduce_scatter | solution.py:317
  322.6 94.2 %reduce-scatter.12.cloned.1.call-start = ((), (), s32[]{:S(2)}) async-start(), calls=%async_computation.12 | async-start | bytes 2949120 | tf_op jit(solution)/shard_map/reduce_scatter | solution.py:308
  324.1 3.1 copy-start.20
  324.1 3.1 copy-start.22
  327.1 154.7 %reduce-scatter.20.cloned.1.call-start = ((), (), s32[]{:S(2)}) async-start(), calls=%async_computation.16 | async-start | bytes 7372800 | tf_op jit(solution)/shard_map/reduce_scatter | solution.py:329
  331.0 216.0 %reduce-scatter.18.cloned.1.call-start = ((), (), s32[]{:S(2)}) async-start(), calls=%async_computation.15 | async-start | bytes 7372800 | tf_op jit(solution)/shard_map/reduce_scatter | solution.py:326
  336.0 275.9 %reduce-scatter.16.cloned.1.call-start = ((), (), s32[]{:S(2)}) async-start(), calls=%async_computation.14 | async-start | bytes 7372800 | tf_op jit(solution)/shard_map/reduce_scatter | solution.py:323
  340.9 470.1 %all-reduce.10.cloned.1.call-start = ((), (), s32[]{:S(2)}) async-start(), calls=%async_computation.19 | async-start | bytes 19988480 | tf_op jit(solution)/shard_map/psum | solution.py:335
  613.5 1.9 copy-start.15
  613.5 2.4 copy-start.17
  615.8 41.3 %copy-start.9 = (f32[192,960]{1,0:T(8,128)S(1)}, f32[192,960]{1,0:T(8,128)}, u32[]{:S(2)}) copy-start(f32[192,960]{1,0:T(8,128)} %copy-done.7) | copy-start | bytes 2211844
  811.1 4.5 copy-start.41
  811.1 4.5 copy-start.42
  811.1 5.8 copy-start.27
  811.1 5.8 copy-start.28
  816.9 2.6 copy-start.18
  816.9 3.9 copy-start.19
  (17 other events, 19.3 us)
Sparse Core Ops, SparseCore 0:
  9.5 46.8 all-gather.7
  58.0 33.0 all-gather.9
  92.6 64.8 all-gather.13
  158.9 64.8 all-gather.11
  225.2 64.8 all-gather.15
  313.9 16.9 reduce-scatter.23
  333.1 16.9 reduce-scatter.21
  353.0 30.4 reduce-scatter.13
  386.3 30.4 reduce-scatter.11
  419.6 62.1 reduce-scatter.19
  484.7 62.1 reduce-scatter.17
  549.7 62.1 reduce-scatter.15
  616.7 194.3 all-reduce.9
where the time goes:
time: 833 us; the launch traced here: 832 us
  waiting for transfers between devices  628 us (75%)
  blocking collectives  79.5 us (10%)
  matrix products  63.8 us (8%)
  local copies, waits for them, and re-layouts  22.6 us (3%)
  other arithmetic  21.1 us (3%)
  between operations  16 us (2%)
    psum x1, waiting for transfers between devices, local(): lax.psum(parts[1].astype(jnp.bfloat16), 'replica').astype(jnp.float32)  149 us
    reduce_scatter x1, waiting for transfers between devices, local(): lax.psum_scatter(mlp_grads[2].astype(jnp.bfloat16), 'group', scatter_dime...  65.1 us
    reduce_scatter x1, waiting for transfers between devices, local(): lax.psum_scatter(mlp_grads[1].astype(jnp.bfloat16), 'group', scatter_dime...  65 us
    reduce_scatter x1, waiting for transfers between devices, local(): lax.psum_scatter(mlp_grads[3].astype(jnp.bfloat16), 'group', scatter_dime...  65 us
    all_gather x1, waiting for transfers between devices, local(): lax.all_gather(w_up, 'group', axis=1, tiled=True)  62.2 us
    all_gather x1, waiting for transfers between devices, local(): lax.all_gather(w_gate, 'group', axis=1, tiled=True)  61.3 us
    all_gather x1, waiting for transfers between devices, local(): lax.all_gather(w_down, 'group', axis=0, tiled=True)  61.3 us
    psum x1, blocking collectives, local(): lax.psum(parts[0].astype(jnp.bfloat16), 'replica').astype(jnp.float32)  33.8 us
  transfers between devices with their start and end apart: 13, of which 11 were waited for; matrix products, arithmetic and copies ran while one was open for 8% of the time, Pallas kernels for 0%

commit v1 on v0

--- a/solution.py
+++ b/solution.py
@@ -332,7 +332,9 @@
     )
     totals = (
         lax.psum(parts[0].astype(jnp.bfloat16), "replica").astype(jnp.float32),
-        lax.psum(parts[1].astype(jnp.bfloat16), "replica").astype(jnp.float32),
+        jnp.sum(lax.all_gather(parts[1].astype(jnp.bfloat16), "replica"), axis=0).astype(
+            jnp.float32
+        ),
         lax.psum(parts[2].astype(jnp.bfloat16), "replica").astype(jnp.float32),
         lax.psum(parts[3].astype(jnp.bfloat16), "replica").astype(jnp.float32),
         lax.psum(parts[4].astype(jnp.bfloat16), "replica").astype(jnp.float32),

time: 833 us -> 936 us (1.12)
  waiting for transfers between devices: 628 us -> 721 us
  other arithmetic: 21.1 us -> 30.6 us
    all_gather x0 -> x1, waiting for transfers between devices: none -> 108 us  [local(): lax.all_gather(parts[1].astype(jnp.bfloat16), 'replica')]
    psum x1, waiting for transfers between devices: 149 us -> 133 us  [local(): lax.psum(parts[2].astype(jnp.bfloat16), 'replica').astype(jnp.float32)]
    unnamed x117 -> x97, local copies, waits for them, and re-layouts: 19.1 us -> 19.7 us
  transfers between devices with their start and end apart: 13 -> 14, of which waited for: 11 -> 12; matrix products, arithmetic and copies ran while one was open for 8% -> 8% of each run, Pallas kernels for 0% -> 0%
where the time goes in v1:
time: 936 us; the launch traced here: 935 us
  waiting for transfers between devices  721 us (77%)
  blocking collectives  79.5 us (8%)
  matrix products  63.9 us (7%)
  other arithmetic  30.6 us (3%)
  local copies, waits for them, and re-layouts  23.8 us (3%)
  between operations  15.8 us (2%)
    psum x1, waiting for transfers between devices, local(): lax.psum(parts[2].astype(jnp.bfloat16), 'replica').astype(jnp.float32)  133 us
    all_gather x1, waiting for transfers between devices, local(): lax.all_gather(parts[1].astype(jnp.bfloat16), 'replica')  108 us
    reduce_scatter x1, waiting for transfers between devices, local(): lax.psum_scatter(mlp_grads[3].astype(jnp.bfloat16), 'group', scatter_dime...  65.1 us
    reduce_scatter x1, waiting for transfers between devices, local(): lax.psum_scatter(mlp_grads[1].astype(jnp.bfloat16), 'group', scatter_dime...  65.1 us
    reduce_scatter x1, waiting for transfers between devices, local(): lax.psum_scatter(mlp_grads[2].astype(jnp.bfloat16), 'group', scatter_dime...  65 us
    all_gather x1, waiting for transfers between devices, local(): lax.all_gather(w_up, 'group', axis=1, tiled=True)  62.2 us
    all_gather x1, waiting for transfers between devices, local(): lax.all_gather(w_gate, 'group', axis=1, tiled=True)  61.3 us
    all_gather x1, waiting for transfers between devices, local(): lax.all_gather(w_down, 'group', axis=0, tiled=True)  61.3 us
  transfers between devices with their start and end apart: 14, of which 12 were waited for; matrix products, arithmetic and copies ran while one was open for 8% of the time, Pallas kernels for 0%

profile of v1, /device:TPU:0, one launch (start us, length us, event | category | flops | bytes accessed | tf_op | source)
XLA Modules:
  0.0 934.7 jit_solution(11415830999854037372)
XLA Ops:
  12.9 5.9 all-reduce.7
  18.8 17.0 %all-gather.2 = bf16[2,480,320]{1,2,0:T(8,128)(2,1)S(1)} all-gather(bf16[1,480,320]{1,2,0:T(8,128)(2,1)S(1)} %bitcast.136), channel_id=1, replica_groups=mesh['group'=2,'replica'=16] {'group'}, dimensions={0}, use_global_device_ids=true | all-gather | bytes 921600 | tf_op jit(solution)/shard_map/all_gather | solution.py:279
  37.1 17.9 %all-gather.1 = bf16[2,480,320]{1,2,0:T(8,128)(2,1)S(1)} all-gather(bf16[1,480,320]{1,2,0:T(8,128)(2,1)S(1)} %bitcast.137), channel_id=1, replica_groups=mesh['group'=2,'replica'=16] {'group'}, dimensions={0}, use_global_device_ids=true | all-gather | bytes 921600 | tf_op jit(solution)/shard_map/all_gather | solution.py:280
  59.7 2.6 fusion.38
  63.2 1.5 fusion.44
  65.2 1.4 fusion.9
  66.6 24.4 %all-gather.12.cloned.1.call-done = bf16[960,960]{1,0:T(8,128)(2,1)} async-done(((bf16[480,960]{1,0:T(8,128)(2,1)}), bf16[960,960]{1,0:T(8,128)(2,1)}) %all-gather.12.cloned.1.call-update) | async-done | bytes 1843216 | tf_op jit(solution)/shard_map/all_gather | solution.py:281
  91.1 2.4 multiply_reduce_fusion.2
  95.3 62.2 %all-gather.16.cloned.1.call-done = bf16[960,2560]{1,0:T(8,128)(2,1)} async-done(((bf16[960,1280]{1,0:T(8,128)(2,1)}), bf16[960,2560]{1,0:T(8,128)(2,1)}) %all-gather.16.cloned.1.call-update) | async-done | bytes 4915216 | tf_op jit(solution)/shard_map/all_gather | solution.py:284
  157.5 5.0 fusion.46
  162.5 61.3 %all-gather.14.cloned.1.call-done = bf16[960,2560]{1,0:T(8,128)(2,1)} async-done(((bf16[960,1280]{1,0:T(8,128)(2,1)}), bf16[960,2560]{1,0:T(8,128)(2,1)}) %all-gather.14.cloned.1.call-update) | async-done | bytes 4915216 | tf_op jit(solution)/shard_map/all_gather | solution.py:283
  223.8 5.0 fusion.45
  228.8 61.3 %all-gather.18.cloned.1.call-done = bf16[2560,960]{0,1:T(8,128)(2,1)} async-done(((bf16[1280,960]{0,1:T(8,128)(2,1)}), bf16[2560,960]{0,1:T(8,128)(2,1)}) %all-gather.18.cloned.1.call-update) | async-done | bytes 4915216 | tf_op jit(solution)/shard_map/all_gather | solution.py:285
  290.1 6.4 multiply_convert_fusion
  296.5 1.6 fusion.47
  298.1 4.2 multiply_reduce_fusion
  304.2 1.5 convolution_convert_fusion.7
  305.7 2.0 copy.65
  307.7 1.9 fusion.14
  311.5 2.2 copy.89
  313.8 1.4 fusion.17
  315.2 1.9 fusion.2
  320.7 1.9 convolution_convert_fusion.3
  322.7 3.7 convolution_convert_fusion
  327.8 3.7 convolution_convert_fusion.1
  332.7 3.7 convolution_convert_fusion.2
  338.4 2.1 convolution_convert_fusion.4
  340.7 1.9 copy.90
  342.5 7.6 reduce-scatter.22.cloned.1.call-done
  350.1 1.9 copy.88
  352.0 31.5 %reduce-scatter.14.cloned.1.call-done = bf16[480,960]{1,0:T(8,128)(2,1)} async-done(((bf16[960,960]{1,0:T(8,128)(2,1)}), bf16[480,960]{1,0:T(8,128)(2,1)}) %reduce-scatter.14.cloned.1.call-update) | async-done | bytes 921616 | tf_op jit(solution)/shard_map/reduce_scatter | solution.py:317
  383.5 65.1 %reduce-scatter.20.cloned.1.call-done = bf16[1280,960]{0,1:T(8,128)(2,1)} async-done(((bf16[2560,960]{0,1:T(8,128)(2,1)}), bf16[1280,960]{0,1:T(8,128)(2,1)}) %reduce-scatter.20.cloned.1.call-update) | async-done | bytes 2457616 | tf_op jit(solution)/shard_map/reduce_scatter | solution.py:329
  448.6 65.0 %reduce-scatter.18.cloned.1.call-done = bf16[960,1280]{1,0:T(8,128)(2,1)} async-done(((bf16[960,2560]{1,0:T(8,128)(2,1)}), bf16[960,1280]{1,0:T(8,128)(2,1)}) %reduce-scatter.18.cloned.1.call-update) | async-done | bytes 2457616 | tf_op jit(solution)/shard_map/reduce_scatter | solution.py:326
  513.6 65.1 %reduce-scatter.16.cloned.1.call-done = bf16[960,1280]{1,0:T(8,128)(2,1)} async-done(((bf16[960,2560]{1,0:T(8,128)(2,1)}), bf16[960,1280]{1,0:T(8,128)(2,1)}) %reduce-scatter.16.cloned.1.call-update) | async-done | bytes 2457616 | tf_op jit(solution)/shard_map/reduce_scatter | solution.py:323
  578.8 33.1 %reduce-scatter.12.cloned.1.call-done = bf16[480,960]{1,0:T(8,128)(2,1)} async-done(((bf16[960,960]{1,0:T(8,128)(2,1)}), bf16[480,960]{1,0:T(8,128)(2,1)}) %reduce-scatter.12.cloned.1.call-update) | async-done | bytes 921616 | tf_op jit(solution)/shard_map/reduce_scatter | solution.py:308
  612.6 2.3 fusion.48
  615.4 1.8 fusion.26
  617.2 4.9 all-reduce.6
  622.3 33.8 %all-reduce.4 = (bf16[480]{0:T(512)(128)(2,1)S(1)}, bf16[480]{0:T(512)(128)(2,1)S(1)}) all-reduce(bf16[480]{0:T(512)(128)(2,1)S(1)} %dynamic-slice.3, bf16[480]{0:T(512)(128)(2,1)S(1)} %dynamic-slice.5), channel_id=1, replica_groups=mesh['group'=2,'replica'=16] {'replica'}, use_global_device_ids=true, to_apply=%region_11.12 | all-reduce | flops 960 | bytes 3840 | tf_op jit(solution)/shard_map/psum | solution.py:334
  657.8 5.1 fusion.10
  662.9 132.8 %all-reduce.10.cloned.1.call-done = (bf16[480,320]{0,1:T(8,128)(2,1)}, bf16[480,320]{0,1:T(8,128)(2,1)}, bf16[480,960]{1,0:T(8,128)(2,1)}, bf16[960,1280]{1,0:T(...) async-done(((bf16[480,320]{0,1:T(8,128)(2,1)}, bf16[480,320]{0,1:T(8,128)(2,1)}, bf16[480,960]{1,0:T(8,128)(2,1)}, bf16[960,1280]{1,0:T(8,128)(2,1)}, ...) | async-done | bytes 8908816 | tf_op jit(solution)/shard_map/psum | solution.py:338
  795.8 2.5 convert_multiply_fusion.11
  798.2 2.7 convert_multiply_fusion.3
  801.0 2.9 convert_multiply_fusion
  805.3 4.7 convert_multiply_fusion.1
  810.0 107.8 %all-gather.20.cloned.1.call-done = bf16[7680,960]{1,0:T(8,128)(2,1)} async-done(((bf16[480,960]{1,0:T(8,128)(2,1)}), bf16[7680,960]{1,0:T(8,128)(2,1)}) %all-gather.20.cloned.1.call-update) | async-done | bytes 14745616 | tf_op jit(solution)/shard_map/all_gather | solution.py:335
  917.8 8.8 reduce_sum.101
  926.6 1.5 convert_multiply_fusion.4
  (161 shorter events, 29.5 us)
Async XLA Ops:
  7.2 52.5 %all-gather.10.cloned.1.call-start = ((), (), s32[]{:S(2)}) async-start(), calls=%async_computation.7 | async-start | bytes 2949120 | tf_op jit(solution)/shard_map/all_gather | solution.py:278
  7.9 83.2 %all-gather.12.cloned.1.call-start = ((), (), s32[]{:S(2)}) async-start(), calls=%async_computation.8 | async-start | bytes 2949120 | tf_op jit(solution)/shard_map/all_gather | solution.py:281
  8.7 148.9 %all-gather.16.cloned.1.call-start = ((), (), s32[]{:S(2)}) async-start(), calls=%async_computation.10 | async-start | bytes 7372800 | tf_op jit(solution)/shard_map/all_gather | solution.py:284
  9.4 1.6 copy-start
  9.4 1.8 copy-start.38
  9.4 3.0 copy-start.39
  9.4 3.3 copy-start.40
  9.4 9.4 %copy-start.36 = (bf16[480,320]{0,1:T(8,128)(2,1)S(1)}, bf16[480,320]{0,1:T(8,128)(2,1)}, u32[]{:S(2)}) copy-start(bf16[480,320]{0,1:T(8,128)(2,1)} %param.17) | copy-start | bytes 921604
  9.5 214.3 %all-gather.14.cloned.1.call-start = ((), (), s32[]{:S(2)}) async-start(), calls=%async_computation.9 | async-start | bytes 7372800 | tf_op jit(solution)/shard_map/all_gather | solution.py:283
  10.0 27.1 %copy-start.37 = (bf16[480,320]{0,1:T(8,128)(2,1)S(1)}, bf16[480,320]{0,1:T(8,128)(2,1)}, u32[]{:S(2)}) copy-start(bf16[480,320]{0,1:T(8,128)(2,1)} %param.18) | copy-start | bytes 921604
  10.0 280.0 %all-gather.18.cloned.1.call-start = ((), (), s32[]{:S(2)}) async-start(), calls=%async_computation.11 | async-start | bytes 7372800 | tf_op jit(solution)/shard_map/all_gather | solution.py:285
  10.6 330.0 %reduce-scatter.24.cloned.1.call-start = ((), (), s32[]{:S(2)}) async-start(), calls=%async_computation.19 | async-start | bytes 1105920
  37.1 22.0 %copy-start.12 = (bf16[960,320]{0,1:T(8,128)(2,1)}, bf16[960,320]{0,1:T(8,128)(2,1)S(1)}, u32[]{:S(2)}) copy-start(bf16[960,320]{0,1:T(8,128)(2,1)S(1)} %reshape.228) | copy-start | bytes 1843204
  56.3 5.9 copy-start.14
  59.7 5.0 copy-start.32
  59.7 3.5 copy-start.34
  62.5 2.2 copy-start.29
  63.2 2.0 copy-start.31
  290.1 6.4 copy-start.2
  296.4 1.7 copy-start.23
  296.4 1.7 copy-start.25
  296.4 1.7 copy-start.8
  298.1 4.2 copy-start.19
  302.4 1.8 copy-start.10
  313.8 36.4 %reduce-scatter.22.cloned.1.call-start = ((), (), s32[]{:S(2)}) async-start(), calls=%async_computation.18 | async-start | bytes 1105920
  313.8 4.5 copy-start.28
  313.8 4.5 copy-start.30
  318.3 2.4 copy-start.6
  318.3 2.4 copy-start.11
  320.6 2.1 copy-start.18
  320.6 2.1 copy-start.20
  320.6 62.9 %reduce-scatter.14.cloned.1.call-start = ((), (), s32[]{:S(2)}) async-start(), calls=%async_computation.13 | async-start | bytes 2949120 | tf_op jit(solution)/shard_map/reduce_scatter | solution.py:317
  322.6 126.0 %reduce-scatter.20.cloned.1.call-start = ((), (), s32[]{:S(2)}) async-start(), calls=%async_computation.16 | async-start | bytes 7372800 | tf_op jit(solution)/shard_map/reduce_scatter | solution.py:329
  326.4 1.3 copy-start.26
  326.5 187.1 %reduce-scatter.18.cloned.1.call-start = ((), (), s32[]{:S(2)}) async-start(), calls=%async_computation.15 | async-start | bytes 7372800 | tf_op jit(solution)/shard_map/reduce_scatter | solution.py:326
  331.6 247.2 %reduce-scatter.16.cloned.1.call-start = ((), (), s32[]{:S(2)}) async-start(), calls=%async_computation.14 | async-start | bytes 7372800 | tf_op jit(solution)/shard_map/reduce_scatter | solution.py:323
  336.5 1.4 copy-start.4
  336.5 1.4 copy-start.33
  336.5 1.4 copy-start.35
  336.5 275.4 %reduce-scatter.12.cloned.1.call-start = ((), (), s32[]{:S(2)}) async-start(), calls=%async_computation.12 | async-start | bytes 2949120 | tf_op jit(solution)/shard_map/reduce_scatter | solution.py:308
  340.6 455.2 %all-reduce.10.cloned.1.call-start = ((), (), s32[]{:S(2)}) async-start(), calls=%async_computation.20 | async-start | bytes 18022400 | tf_op jit(solution)/shard_map/psum | solution.py:338
  578.7 36.2 %copy-start.13 = (bf16[960,320]{0,1:T(8,128)(2,1)S(1)}, bf16[960,320]{0,1:T(8,128)(2,1)}, u32[]{:S(2)}) copy-start(bf16[960,320]{0,1:T(8,128)(2,1)} %copy-done.12) | copy-start | bytes 1843204
  578.7 339.0 %all-gather.20.cloned.1.call-start = ((), (), s32[]{:S(2)}) async-start(), calls=%async_computation.17 | async-start | bytes 16711680 | tf_op jit(solution)/shard_map/all_gather | solution.py:335
  611.9 3.5 copy-start.22
  615.4 42.4 %copy-start.9 = (f32[192,960]{1,0:T(8,128)S(1)}, f32[192,960]{1,0:T(8,128)}, u32[]{:S(2)}) copy-start(f32[192,960]{1,0:T(8,128)} %copy-done.7) | copy-start | bytes 2211844
  795.8 5.2 copy-start.17
  801.0 2.9 copy-start.15
  801.0 4.3 copy-start.16
  (8 other events, 7.8 us)
Sparse Core Ops, SparseCore 0:
  9.5 46.8 all-gather.9
  58.0 33.0 all-gather.11
  92.6 64.8 all-gather.15
  158.9 64.8 all-gather.13
  225.2 64.8 all-gather.17
  313.9 16.9 reduce-scatter.23
  333.1 16.9 reduce-scatter.21
  353.0 30.4 reduce-scatter.13
  386.4 62.1 reduce-scatter.19
  451.3 62.1 reduce-scatter.17
  516.5 62.1 reduce-scatter.15
  581.4 30.4 reduce-scatter.11
  616.4 179.2 all-reduce.9
  797.9 119.8 all-gather.19
